TPU v7x, 128 devices: a whole 4x4x4 slice. The times are simulated.
128 devices in a mesh: row: 16 (over y_lo, x, core), col: 8 (over y_hi, z).
Axes of the slice: x: 4, y: 4 (y_hi: 2, y_lo: 2; y = y_hi * 2 + y_lo), z: 4, core: 2. Of those that a mesh axis runs over, the one named last changes fastest.
Arguments:
- embeddings: float32 [49152, 64], P(('row', 'col')), may hold values from -6 to 6
- inv_length: float32 [64], replicated, may hold values from 0.1 to 0.4
- noise: float32 [49152], P(('row', 'col')), may hold values from 0.1 to 1
- probes: bfloat16 [49152, 256], P(('row', 'col')), may hold values from -1.5 to 1.5
Outputs:
- applied: float32 [49152, 256], P(('row', 'col'))
All inputs are finite; a program needn't handle non-finite values.
Results may differ from a plain program's by a relative error of at most 0.0029.
Values may be sent and summed in bfloat16 or wider, within the bound.
No kernel may reach another device: no remote copies, remote signals or barrier semaphores. Data moves between devices by JAX's collectives and lax.ppermute only.
A program may use at most 192 MiB of HBM per device.

v0:
```python
import jax
import jax.numpy as jnp
from jax import lax
from jax.sharding import PartitionSpec as P


def kernel_tile(rows, row_sq, cols, col_sq, col_probes):
    gram = jnp.dot(
        rows, cols.T, precision=lax.Precision.HIGHEST, preferred_element_type=jnp.float32
    )
    dist = row_sq[:, None] + col_sq[None, :] - 2.0 * gram
    kernel = jnp.exp(-0.5 * dist).astype(jnp.bfloat16)
    return jnp.dot(kernel, col_probes, preferred_element_type=jnp.float32)


def on_device(embeddings, inv_length, noise, probes):
    scaled = embeddings * inv_length[None, :]
    own_sq = jnp.sum(scaled * scaled, axis=1)
    diag_term = noise[:, None] * probes.astype(jnp.float32)
    every = lax.all_gather(scaled, ("row", "col"), axis=0, tiled=True)
    every_sq = jnp.sum(every * every, axis=1)
    product = kernel_tile(
        scaled, own_sq, every, every_sq, lax.all_gather(probes, ("row", "col"), axis=0, tiled=True)
    )
    return product + diag_term


def solution(mesh):
    return jax.shard_map(
        on_device,
        mesh=mesh,
        in_specs=(P(("row", "col"), None), P(), P(("row", "col")), P(("row", "col"), None)),
        out_specs=P(("row", "col"), None),
        check_vma=False,
    )
```

profile of v0, /device:TPU:1, one launch (start us, length us, event | category | flops | bytes accessed | tf_op | source)
XLA Modules:
  0.0 696.6 jit_solution(2096074242026698704)
XLA Ops:
  6.5 0.0 all-gather.3.cloned.1.call-start
  6.5 1.6 multiply_reduce_fusion.1
  8.2 0.0 all-gather.3.cloned.1.call-update
  8.2 0.0 all-gather.5.cloned.1.call-start
  8.2 0.7 all-gather.5.cloned.1.call-update
  8.9 321.8 %all-gather.3.cloned.1.call-done = f32[49152,64]{0,1:T(8,128)} async-done(((f32[384,64]{0,1:T(8,128)}), f32[49152,64]{0,1:T(8,128)}) %all-gather.3.cloned.1.call-update) | async-done | bytes 12582928 | tf_op jit(solution)/shard_map/all_gather | solution.py:20
  330.7 5.8 multiply_reduce_fusion
  336.5 0.0 copy-start
  336.5 0.0 copy-start.1
  336.5 77.5 %exponential_convert_fusion = bf16[384,49152]{1,0:T(8,128)(2,1)} fusion(f32[384,64]{0,1:T(8,128)} %get-tuple-element.6, f32[49152,64]{0,1:T(8,128)} %all-gather.3.cloned.1.call-done, f32[49152]{0:T(1024)S(1)} %multiply_reduce_fusion, f32[384]{0:T(512)S(1)} %get-tuple-element.5), kind=kOutput, calls=%fused_computation | convolution fusion | flops 14589886464 | bytes 50628096 | tf_op jit(solution)/shard_map/dot_general | solution.py:8
  414.1 251.7 %all-gather.5.cloned.1.call-done = bf16[49152,256]{1,0:T(8,128)(2,1)} async-done(((bf16[384,256]{1,0:T(8,128)(2,1)}), bf16[49152,256]{1,0:T(8,128)(2,1)}) %all-gather.5.cloned.1.call-update) | async-done | bytes 25165840 | tf_op jit(solution)/shard_map/all_gather | solution.py:23
  665.8 0.0 copy-done
  665.8 0.0 copy-done.1
  665.8 24.0 %convolution_add_fusion = f32[384,256]{1,0:T(8,128)} fusion(bf16[384,49152]{1,0:T(8,128)(2,1)} %exponential_convert_fusion, bf16[49152,256]{1,0:T(8,128)(2,1)} %all-gather.5.cloned.1.call-done, bf16[384,256]{1,0:T(8,128)(2,1)S(1)} %copy-done, f32[384]{0:T(512)S(1)} %copy-done.1), kind=kOutput, calls=%fused_computation.2 | convolution fusion | flops 9663971328 | bytes 63505920 | tf_op jit(solution)/shard_map/dot_general | solution.py:13
Async XLA Ops:
  6.5 324.2 %all-gather.3.cloned.1.call-start = ((), (), s32[]{:S(2)}) async-start(), calls=%async_computation | async-start | bytes 12681216 | tf_op jit(solution)/shard_map/all_gather | solution.py:20
  8.2 657.6 %all-gather.5.cloned.1.call-start = ((), (), s32[]{:S(2)}) async-start(), calls=%async_computation.1 | async-start | bytes 25362432 | tf_op jit(solution)/shard_map/all_gather | solution.py:23
  336.5 329.3 %copy-start = (bf16[384,256]{1,0:T(8,128)(2,1)S(1)}, bf16[384,256]{1,0:T(8,128)(2,1)}, u32[]{:S(2)}) copy-start(bf16[384,256]{1,0:T(8,128)(2,1)} %param.7) | copy-start | bytes 589828
  336.5 329.2 %copy-start.1 = (f32[384]{0:T(512)S(1)}, f32[384]{0:T(512)}, u32[]{:S(2)}) copy-start(f32[384]{0:T(512)} %param.6) | copy-start | bytes 4612
Sparse Core Ops, SparseCore 0:
  9.0 321.6 all-gather.2
  332.4 333.2 all-gather.4
where the time goes:
time: 697 us
  waiting for transfers between devices  574 us (82%)
  matrix products  102 us (15%)
  between operations  13.4 us (2%)
  other arithmetic  7.37 us (1%)
    all_gather x1, waiting for transfers between devices, on_device(): every = lax.all_gather(scaled, ('row', 'col'), axis=0, tiled=True)  322 us
    all_gather x1, waiting for transfers between devices, on_device(): lax.all_gather(probes, ('row', 'col'), axis=0, tiled=True)  252 us
    dot_general x1, matrix products, kernel_tile(): jnp.dot(rows, cols.T, precision=lax.Precision.HIGHEST, preferred_element_...  77.5 us
    dot_general x1, matrix products, kernel_tile(): return jnp.dot(kernel, col_probes, preferred_element_type=jnp.float32)  24 us
  transfers between devices with their start and end apart: 2, of which 2 were waited for; matrix products, arithmetic and copies ran while one was open for 12% of the time, Pallas kernels for 0%

commit v1 on v0

--- a/solution.py
+++ b/solution.py
@@ -17,7 +17,10 @@
     scaled = embeddings * inv_length[None, :]
     own_sq = jnp.sum(scaled * scaled, axis=1)
     diag_term = noise[:, None] * probes.astype(jnp.float32)
-    every = lax.all_gather(scaled, ("row", "col"), axis=0, tiled=True)
+    every = jnp.concatenate(
+        lax.all_to_all(jnp.stack([scaled] * lax.axis_size(("row", "col"))), ("row", "col"), 0, 0),
+        axis=0,
+    )
     every_sq = jnp.sum(every * every, axis=1)
     product = kernel_tile(
         scaled, own_sq, every, every_sq, lax.all_gather(probes, ("row", "col"), axis=0, tiled=True)

time: 697 us -> 506 us (0.73)
  waiting for transfers between devices: 574 us -> 202 us
  blocking collectives: 0 us -> 167 us
  local copies, waits for them, and re-layouts: 0.01 us -> 11.5 us
    all_gather x1 -> x0, waiting for transfers between devices: 322 us -> none  [on_device(): every = lax.all_gather(scaled, ('row', 'col'), axis=0, tiled=True)]
    all_to_all x0 -> x1, blocking collectives: none -> 167 us  [on_device(): lax.all_to_all(jnp.stack([scaled] * lax.axis_size(('row', 'col'))), ('row...]
    all_gather x1, waiting for transfers between devices: 252 us -> 202 us  [on_device(): lax.all_gather(probes, ('row', 'col'), axis=0, tiled=True)]
    reshape x0 -> x1, local copies, waits for them, and re-layouts: none -> 9.89 us  [on_device(): jnp.concatenate(lax.all_to_all(jnp.stack([scaled] * lax.axis_size(('row',...]
  transfers between devices with their start and end apart: 2 -> 1, of which waited for: 2 -> 1; matrix products, arithmetic and copies ran while one was open for 12% -> 19% of each run, Pallas kernels for 0% -> 0%
where the time goes in v1:
time: 506 us; the launch traced here: 504 us
  waiting for transfers between devices  202 us (40%)
  blocking collectives  167 us (33%)
  matrix products  102 us (20%)
  between operations  13.4 us (3%)
  local copies, waits for them, and re-layouts  11.5 us (2%)
  other arithmetic  7.86 us (2%)
    all_gather x1, waiting for transfers between devices, on_device(): lax.all_gather(probes, ('row', 'col'), axis=0, tiled=True)  202 us
    all_to_all x1, blocking collectives, on_device(): lax.all_to_all(jnp.stack([scaled] * lax.axis_size(('row', 'col'))), ('row...  167 us
    dot_general x1, matrix products, kernel_tile(): jnp.dot(rows, cols.T, precision=lax.Precision.HIGHEST, preferred_element_...  77.7 us
    dot_general x1, matrix products, kernel_tile(): return jnp.dot(kernel, col_probes, preferred_element_type=jnp.float32)  24 us
  transfers between devices with their start and end apart: 1, of which 1 were waited for; matrix products, arithmetic and copies ran while one was open for 19% of the time, Pallas kernels for 0%

profile of v1, /device:TPU:1, one launch (start us, length us, event | category | flops | bytes accessed | tf_op | source)
XLA Modules:
  0.0 504.0 jit_solution(4785490584450723699)
XLA Ops:
  6.5 0.0 all-gather.2.cloned.1.call-start
  6.5 0.7 all-gather.2.cloned.1.call-update
  7.3 1.0 multiply_reduce_fusion.1
  8.2 1.6 stack.2
  9.8 167.0 %all_to_all.5 = f32[128,384,64]{1,2,0:T(8,128)} all-to-all(f32[128,384,64]{1,2,0:T(8,128)S(1)} %stack.2), channel_id=1, replica_groups=mesh['row'=16,'col'=8] {'row','col'}, dimensions={0} | all-to-all | bytes 25165824 | tf_op jit(solution)/shard_map/all_to_all | solution.py:21
  176.9 9.9 %copy.7 = f32[128,8,8,384]{3,2,0,1:T(8,128)} copy(f32[128,8,8,384]{3,2,1,0:T(8,128)} %bitcast.6) | data formatting | bytes 25165824 | tf_op jit(solution)/shard_map/reshape | solution.py:20
  186.7 6.9 %multiply_reduce_fusion = f32[128,384]{1,0:T(8,128)S(1)} fusion(f32[128,384,64]{1,2,0:T(8,128)} %all_to_all.5), kind=kLoop, calls=%fused_computation.1 | loop fusion | flops 6242304 | bytes 12779520 | tf_op jit(solution)/shard_map/reduce_sum | solution.py:24
  193.6 0.0 copy-start
  193.7 0.0 copy-start.1
  193.7 77.7 %exponential_convert_fusion = bf16[384,49152]{1,0:T(8,128)(2,1)} fusion(f32[384,64]{0,1:T(8,128)S(1)} %get-tuple-element.6, f32[49152,64]{0,1:T(8,128)} %bitcast.7, f32[49152]{0:T(1024)S(1)} %add.19, f32[384]{0:T(512)S(1)} %get-tuple-element.5), kind=kOutput, calls=%fused_computation | convolution fusion | flops 14589886464 | bytes 50628096 | tf_op jit(solution)/shard_map/dot_general | solution.py:8
  271.4 201.7 %all-gather.2.cloned.1.call-done = bf16[49152,256]{1,0:T(8,128)(2,1)} async-done(((bf16[384,256]{1,0:T(8,128)(2,1)}), bf16[49152,256]{1,0:T(8,128)(2,1)}) %all-gather.2.cloned.1.call-update) | async-done | bytes 25165840 | tf_op jit(solution)/shard_map/all_gather | solution.py:26
  473.1 0.0 copy-done
  473.1 0.0 copy-done.1
  473.1 24.0 %convolution_add_fusion = f32[384,256]{1,0:T(8,128)} fusion(bf16[384,49152]{1,0:T(8,128)(2,1)} %exponential_convert_fusion, bf16[49152,256]{1,0:T(8,128)(2,1)} %all-gather.2.cloned.1.call-done, bf16[384,256]{1,0:T(8,128)(2,1)S(1)} %copy-done, f32[384]{0:T(512)S(1)} %copy-done.1), kind=kOutput, calls=%fused_computation.2 | convolution fusion | flops 9663971328 | bytes 63505920 | tf_op jit(solution)/shard_map/dot_general | solution.py:13
  (1 shorter events, 0.0 us)
Async XLA Ops:
  6.5 466.5 %all-gather.2.cloned.1.call-start = ((), (), s32[]{:S(2)}) async-start(), calls=%async_computation.1 | async-start | bytes 25362432 | tf_op jit(solution)/shard_map/all_gather | solution.py:26
  193.6 279.4 %copy-start = (bf16[384,256]{1,0:T(8,128)(2,1)S(1)}, bf16[384,256]{1,0:T(8,128)(2,1)}, u32[]{:S(2)}) copy-start(bf16[384,256]{1,0:T(8,128)(2,1)} %param.7) | copy-start | bytes 589828
  193.7 279.4 %copy-start.1 = (f32[384]{0:T(512)S(1)}, f32[384]{0:T(512)}, u32[]{:S(2)}) copy-start(f32[384]{0:T(512)} %param.6) | copy-start | bytes 4612
Sparse Core Ops, SparseCore 0:
  9.0 464.0 all-gather.1
